TPU v7x, 32 devices: a whole 2x2x4 slice. The times are simulated.
32 devices in a mesh: groups: 2 (over y), row: 8 (over z, x), section: 2 (over core).
Axes of the slice: x: 2, y: 2, z: 4, core: 2. Of those that a mesh axis runs over, the one named last changes fastest.
Arguments:
- hidden: bfloat16 [64, 8192], P('groups', ('row', 'section')), parts along dimension 0, may hold values from -6 to 6
- norm_in_gain: float32 [8192], replicated, may hold values from 0.1 to 1.9
- zx_weight: bfloat16 [8192, 2, 8, 64], P(None, None, 'row', 'section'), may hold values from -0.0625 to 0.0625
- bc_weight: bfloat16 [8192, 2048], P(None, ('row', 'section')), may hold values from -0.0625 to 0.0625
- dt_weight: bfloat16 [8192, 8], P(None, 'row'), may hold values from -0.0625 to 0.0625
- dt_bias: float32 [8], P('row'), may hold values from -3 to -0.5
- decay_log: float32 [8], P('row'), may hold values from -0.7 to 2
- skip_gain: float32 [8], P('row'), may hold values from 0.5 to 1.5
- conv_x_weight: float32 [4, 8, 64], P(None, 'row', 'section'), may hold values from -3.6 to 3.6
- conv_x_bias: float32 [8, 64], P('row', 'section'), may hold values from -3 to 3
- conv_bc_weight: float32 [4, 2048], P(None, ('row', 'section')), may hold values from -3 to 3
- conv_bc_bias: float32 [2048], P(('row', 'section')), may hold values from -3 to 3
- conv_x_state: bfloat16 [64, 3, 8, 64], P('groups', None, 'row', 'section'), parts along dimension 0, may hold values from -6 to 6
- conv_bc_state: bfloat16 [64, 3, 2048], P('groups', None, ('row', 'section')), parts along dimension 0, may hold values from -6 to 6
- ssm_state: bfloat16 [64, 8, 64, 256], P('groups', 'row', 'section'), parts along dimension 0, may hold values from -6 to 6
- gate_norm_weight: float32 [8, 64], P('row', 'section'), may hold values from 0.1 to 1.9
- out_weight: bfloat16 [8, 64, 8192], P('row', 'section'), may hold values from -0.375 to 0.375
- norm_mid_gain: float32 [8192], replicated, may hold values from 0.1 to 1.9
- up_weight: bfloat16 [8192, 16384], P(None, ('row', 'section')), may hold values from -0.0625 to 0.0625
- down_weight: bfloat16 [16384, 8192], P(('row', 'section')), may hold values from -0.0625 to 0.0625
- valid: int32 [64], P('groups'), parts along dimension 0, may hold values 0 or 1
Outputs:
- block_out: bfloat16 [64, 8192], P('groups', ('row', 'section')), parts along dimension 0
- new_ssm_state: bfloat16 [64, 8, 64, 256], P('groups', 'row', 'section'), parts along dimension 0
- new_conv_x_state: bfloat16 [64, 3, 8, 64], P('groups', None, 'row', 'section'), parts along dimension 0
- new_conv_bc_state: bfloat16 [64, 3, 2048], P('groups', None, ('row', 'section')), parts along dimension 0
There are 2 independent parts, one for each index of `groups`. A program takes and returns all parts, laid end to end along the dimension named above; an argument that names none is the same for every part. Nothing has to cross between parts.
All inputs are finite; a program needn't handle non-finite values.
Results may differ from a plain program's by a relative error of at most 0.0075.
Values may be sent and summed in bfloat16 or wider, within the bound.
A program may use at most 128 MiB of HBM per device.

v0:
```python
import jax
import jax.numpy as jnp
from jax import lax
from jax.sharding import PartitionSpec as P

D = 8192
HEAD_DIM = 64
STATE = 256
GROUPS = 4


def mean_norm(values, gain):
    return values * lax.rsqrt(jnp.mean(values * values, axis=-1, keepdims=True) + 1e-05) * gain


def body(
    hidden,
    norm_in_gain,
    zx_weight,
    bc_weight,
    dt_weight,
    dt_bias,
    decay_log,
    skip_gain,
    conv_x_weight,
    conv_x_bias,
    conv_bc_weight,
    conv_bc_bias,
    conv_x_state,
    conv_bc_state,
    ssm_state,
    gate_norm_weight,
    out_weight,
    norm_mid_gain,
    up_weight,
    down_weight,
    valid,
):
    row_count = hidden.shape[0]
    local_p = zx_weight.shape[3]
    full_rows = lax.all_gather(hidden, ("row", "section"), axis=1, tiled=True)
    normed = mean_norm(full_rows.astype(jnp.float32), norm_in_gain).astype(jnp.bfloat16)
    gate_inner = jnp.dot(
        normed, zx_weight.reshape(D, 2 * local_p), preferred_element_type=jnp.float32
    ).reshape(row_count, 2, 1, local_p)
    gate_part = gate_inner[:, 0]
    inner_pre = gate_inner[:, 1].astype(jnp.bfloat16)
    bc_pre = jnp.dot(normed, bc_weight, preferred_element_type=jnp.float32).astype(jnp.bfloat16)
    dt_raw = jnp.dot(normed, dt_weight, preferred_element_type=jnp.float32)
    taps_x = jnp.concatenate([conv_x_state, inner_pre[:, None]], axis=1)
    inner = jax.nn.silu(
        jnp.sum(taps_x.astype(jnp.float32) * conv_x_weight[None], axis=1) + conv_x_bias
    )
    taps_bc = jnp.concatenate([conv_bc_state, bc_pre[:, None]], axis=1)
    mixed_bc = jax.nn.silu(
        jnp.sum(taps_bc.astype(jnp.float32) * conv_bc_weight[None], axis=1) + conv_bc_bias
    )
    all_bc = lax.all_gather(mixed_bc, ("row", "section"), axis=1, tiled=True)
    per_group = lax.axis_size("row") // GROUPS
    group_index = lax.axis_index("row") // per_group
    state_in = all_bc[:, : GROUPS * STATE].reshape(row_count, GROUPS, STATE)
    state_out = all_bc[:, GROUPS * STATE :].reshape(row_count, GROUPS, STATE)
    in_mine = lax.dynamic_slice_in_dim(state_in, group_index, 1, axis=1)
    out_mine = lax.dynamic_slice_in_dim(state_out, group_index, 1, axis=1)
    step_size = jax.nn.softplus(dt_raw + dt_bias[None])
    decay_rate = jnp.exp(-step_size * jnp.exp(decay_log)[None])
    previous = ssm_state.astype(jnp.float32)
    updated = (
        decay_rate[:, :, None, None] * previous
        + (step_size[:, :, None] * inner)[..., None] * in_mine[:, :, None, :]
    )
    readout = (
        jnp.einsum("rhpn,rhn->rhp", updated, out_mine, precision=lax.Precision.HIGHEST)
        + skip_gain[None, :, None] * inner
    )
    gated = readout * jax.nn.silu(gate_part)
    local_squares = jnp.sum(gated * gated, axis=(1, 2))
    group_pick = (jnp.arange(GROUPS) == group_index).astype(jnp.float32)
    group_sums = lax.psum(local_squares[:, None] * group_pick[None], ("row", "section"))
    group_size = per_group * HEAD_DIM
    group_mean = jnp.sum(group_sums * group_pick[None], axis=1) / group_size
    scaled = (gated * lax.rsqrt(group_mean + 1e-05)[:, None, None] * gate_norm_weight[None]).astype(
        jnp.bfloat16
    )
    mixer_terms = jnp.dot(
        scaled.reshape(row_count, local_p),
        out_weight.reshape(local_p, D),
        preferred_element_type=jnp.float32,
    )
    mixer_share = lax.psum_scatter(mixer_terms, ("row", "section"), scatter_dimension=1, tiled=True)
    middle = (hidden.astype(jnp.float32) + mixer_share).astype(jnp.bfloat16)
    middle_full = lax.all_gather(middle, ("row", "section"), axis=1, tiled=True)
    mlp_in = mean_norm(middle_full.astype(jnp.float32), norm_mid_gain).astype(jnp.bfloat16)
    up_values = jnp.dot(mlp_in, up_weight, preferred_element_type=jnp.float32)
    activated = jnp.square(jax.nn.relu(up_values)).astype(jnp.bfloat16)
    down_terms = jnp.dot(activated, down_weight, preferred_element_type=jnp.float32)
    down_share = lax.psum_scatter(down_terms, ("row", "section"), scatter_dimension=1, tiled=True)
    block_out = (middle.astype(jnp.float32) + down_share).astype(jnp.bfloat16)
    kept_rows = valid != 0
    new_ssm_state = jnp.where(kept_rows[:, None, None, None], updated, previous).astype(
        jnp.bfloat16
    )
    new_conv_x_state = jnp.where(kept_rows[:, None, None, None], taps_x[:, 1:], conv_x_state)
    new_conv_bc_state = jnp.where(kept_rows[:, None, None], taps_bc[:, 1:], conv_bc_state)
    return (block_out, new_ssm_state, new_conv_x_state, new_conv_bc_state)


def solution(mesh):
    return jax.shard_map(
        body,
        mesh=mesh,
        in_specs=(
            P("groups", ("row", "section")),
            P(),
            P(None, None, "row", "section"),
            P(None, ("row", "section")),
            P(None, "row"),
            P("row"),
            P("row"),
            P("row"),
            P(None, "row", "section"),
            P("row", "section"),
            P(None, ("row", "section")),
            P(("row", "section")),
            P("groups", None, "row", "section"),
            P("groups", None, ("row", "section")),
            P("groups", "row", "section", None),
            P("row", "section"),
            P("row", "section", None),
            P(),
            P(None, ("row", "section")),
            P(("row", "section"), None),
            P("groups"),
        ),
        out_specs=(
            P("groups", ("row", "section")),
            P("groups", "row", "section", None),
            P("groups", None, "row", "section"),
            P("groups", None, ("row", "section")),
        ),
        check_vma=False,
    )
```

profile of v0, /device:TPU:0, one launch (start us, length us, event | category | flops | bytes accessed | tf_op | source)
XLA Modules:
  0.0 251.6 jit_solution(10273601416538449090)
XLA Ops:
  7.2 0.0 copy-start
  7.2 0.0 reduce-scatter.3.cloned.1.call-start
  7.3 24.9 %all_gather.9 = bf16[32,8192]{1,0:T(8,128)(2,1)S(1)} all-gather(bf16[32,512]{1,0:T(8,128)(2,1)} %param.21), channel_id=1, replica_groups=mesh['groups'=2,'row'=8,'section'=2] {'row','section'}, dimensions={1}, use_global_device_ids=true | all-gather | bytes 557056 | tf_op jit(solution)/shard_map/all_gather | solution.py:41
  32.2 0.2 fusion.4
  32.4 1.7 convolution_bitcast_fusion
  34.2 0.1 copy.32
  34.3 0.8 multiply_reduce_fusion.1
  35.0 0.1 copy.33
  35.8 0.0 copy-done
  35.8 1.2 fusion.2
  37.0 0.8 multiply_reduce_fusion
  37.8 0.7 divide_multiply_fusion
  38.4 18.1 %all_gather.10 = f32[32,2048]{1,0:T(8,128)S(1)} all-gather(f32[32,128]{1,0:T(8,128)S(1)} %divide_multiply_fusion), channel_id=1, replica_groups=mesh['groups'=2,'row'=8,'section'=2] {'row','section'}, dimensions={1}, use_global_device_ids=true | all-gather | bytes 278528 | tf_op jit(solution)/shard_map/all_gather | solution.py:58
  56.6 0.1 reshape.225
  58.1 1.1 multiply_exponential_fusion
  59.2 0.8 broadcast_multiply_fusion
  60.0 0.1 copy.34
  60.0 0.1 reshape.227
  60.1 2.3 fusion.13
  62.3 0.1 copy.36
  62.4 0.8 multiply_reduce_fusion.2
  63.2 0.1 broadcast_multiply_fusion.1
  63.3 31.1 %psum.7 = f32[32,4]{0,1:T(4,128)S(1)} all-reduce(f32[32,4]{0,1:T(4,128)S(1)} %broadcast_multiply_fusion.1), channel_id=1, replica_groups=mesh['groups'=2,'row'=8,'section'=2] {'row','section'}, use_global_device_ids=true, to_apply=%region_4.5 | all-reduce | flops 128 | bytes 1024 | tf_op jit(solution)/shard_map/psum | solution.py:79
  94.4 0.1 multiply_reduce_fusion.3
  94.5 2.5 fusion.19
  96.9 0.0 reduce-scatter.3.cloned.1.call-update
  96.9 0.0 reduce-scatter.5.cloned.1.call-start
  97.0 54.8 %reduce-scatter.3.cloned.1.call-done = f32[32,512]{1,0:T(8,128)} async-done(((f32[32,8192]{1,0:T(8,128)}), f32[32,512]{1,0:T(8,128)}) %reduce-scatter.3.cloned.1.call-update) | async-done | bytes 65552 | tf_op jit(solution)/shard_map/reduce_scatter | solution.py:90
  151.8 0.8 add_convert_fusion.1
  152.6 20.8 %all_gather.11 = bf16[32,8192]{1,0:T(8,128)(2,1)S(1)} all-gather(bf16[32,512]{1,0:T(8,128)(2,1)S(1)} %add_convert_fusion.1), channel_id=1, replica_groups=mesh['groups'=2,'row'=8,'section'=2] {'row','section'}, dimensions={1}, use_global_device_ids=true | all-gather | bytes 557056 | tf_op jit(solution)/shard_map/all_gather | solution.py:92
  173.5 0.2 fusion.9
  173.7 0.0 copy-start.4
  173.7 0.0 copy-start.2
  173.7 0.0 copy-start.3
  173.7 0.0 copy-start.1
  173.7 14.8 %fusion.16 = f32[32,8192]{1,0:T(8,128)} fusion(bf16[1024,8192]{1,0:T(8,128)(2,1)} %param.40, bf16[8192,1024]{1,0:T(8,128)(2,1)} %param.39, bf16[32,8192]{1,0:T(8,128)(2,1)S(1)} %all_gather.11, f32[8192]{0:T(1024)} %param.38, f32[32]{0:T(128)S(1)} %add_rsqrt_fusion), kind=kOutput, calls=%fused_computation.25 | convolution fusion | flops 1074888704 | bytes 35160192 | tf_op jit(solution)/shard_map/dot_general | solution.py:96
  188.5 0.0 reduce-scatter.5.cloned.1.call-update
  188.5 0.0 copy-done.4
  188.5 0.0 copy-done.2
  188.6 0.7 fusion.35
  189.2 0.0 copy-done.3
  189.2 0.7 fusion.33
  189.9 0.0 copy-done.1
  189.9 1.2 fusion.8
  191.1 52.2 %reduce-scatter.5.cloned.1.call-done = f32[32,512]{1,0:T(8,128)} async-done(((f32[32,8192]{1,0:T(8,128)}), f32[32,512]{1,0:T(8,128)}) %reduce-scatter.5.cloned.1.call-update) | async-done | bytes 65552 | tf_op jit(solution)/shard_map/reduce_scatter | solution.py:97
  243.3 1.5 add_convert_fusion
  (9 shorter events, 0.1 us)
Async XLA Ops:
  7.2 28.6 %copy-start = (bf16[8192,128]{1,0:T(8,128)(2,1)S(1)}, bf16[8192,128]{1,0:T(8,128)(2,1)}, u32[]{:S(2)}) copy-start(bf16[8192,128]{1,0:T(8,128)(2,1)} %param.24) | copy-start | bytes 6291460
  7.2 144.6 %reduce-scatter.3.cloned.1.call-start = ((), (), s32[]{:S(2)}) async-start(), calls=%async_computation.2 | async-start | bytes 1114112 | tf_op jit(solution)/shard_map/reduce_scatter | solution.py:90
  96.9 146.4 %reduce-scatter.5.cloned.1.call-start = ((), (), s32[]{:S(2)}) async-start(), calls=%async_computation.3 | async-start | bytes 1114112 | tf_op jit(solution)/shard_map/reduce_scatter | solution.py:97
  173.7 14.8 %copy-start.4 = (s32[32]{0:T(128)S(1)}, s32[32]{0:T(128)}, u32[]{:S(2)}) copy-start(s32[32]{0:T(128)} %param.41) | copy-start | bytes 388
  173.7 14.8 %copy-start.2 = (bf16[32,3,1,32]{3,0,2,1:T(8,128)(2,1)S(1)}, bf16[32,3,1,32]{3,0,2,1:T(8,128)(2,1)}, u32[]{:S(2)}) copy-start(bf16[32,3,1,32]{3,0,2,1:T(8,128)(2,1)} %param.33) | copy-start | bytes 18436
  173.7 15.5 %copy-start.3 = (bf16[32,3,128]{2,0,1:T(8,128)(2,1)S(1)}, bf16[32,3,128]{2,0,1:T(8,128)(2,1)}, u32[]{:S(2)}) copy-start(bf16[32,3,128]{2,0,1:T(8,128)(2,1)} %param.34) | copy-start | bytes 73732
  173.7 16.2 %copy-start.1 = (bf16[32,1,32,256]{3,2,1,0:T(8,128)(2,1)S(1)}, bf16[32,1,32,256]{3,2,1,0:T(8,128)(2,1)}, u32[]{:S(2)}) copy-start(bf16[32,1,32,256]{3,2,1,0:T(8,128)(2,1)} %param.35) | copy-start | bytes 1572868
Sparse Core Ops, SparseCore 0:
  97.1 54.6 reduce-scatter.2
  188.6 54.6 reduce-scatter.4
where the time goes:
time: 252 us
  waiting for transfers between devices  107 us (42%)
  blocking collectives  95 us (38%)
  matrix products  23.5 us (9%)
  between operations  16.2 us (6%)
  other arithmetic  9.25 us (4%)
    reduce_scatter x1, waiting for transfers between devices, body(): lax.psum_scatter(mixer_terms, ('row', 'section'), scatter_dimension=1, ti...  54.8 us
    reduce_scatter x1, waiting for transfers between devices, body(): lax.psum_scatter(down_terms, ('row', 'section'), scatter_dimension=1, til...  52.2 us
    psum x1, blocking collectives, body(): lax.psum(local_squares[:, None] * group_pick[None], ('row', 'section'))  31.1 us
    all_gather x1, blocking collectives, body(): full_rows = lax.all_gather(hidden, ('row', 'section'), axis=1, tiled=True)  24.9 us
    all_gather x1, blocking collectives, body(): middle_full = lax.all_gather(middle, ('row', 'section'), axis=1, tiled=True)  20.8 us
    all_gather x1, blocking collectives, body(): all_bc = lax.all_gather(mixed_bc, ('row', 'section'), axis=1, tiled=True)  18.1 us
    dot_general x1, matrix products, body(): jnp.dot(activated, down_weight, preferred_element_type=jnp.float32)  14.8 us
  transfers between devices with their start and end apart: 2, of which 2 were waited for; matrix products, arithmetic and copies ran while one was open for 1% of the time, Pallas kernels for 0%

commit v1 on v0

--- a/solution.py
+++ b/solution.py
@@ -76,7 +76,7 @@
     gated = readout * jax.nn.silu(gate_part)
     local_squares = jnp.sum(gated * gated, axis=(1, 2))
     group_pick = (jnp.arange(GROUPS) == group_index).astype(jnp.float32)
-    group_sums = lax.psum(local_squares[:, None] * group_pick[None], ("row", "section"))
+    group_sums = lax.psum(lax.psum(local_squares[:, None] * group_pick[None], "section"), "row")
     group_size = per_group * HEAD_DIM
     group_mean = jnp.sum(group_sums * group_pick[None], axis=1) / group_size
     scaled = (gated * lax.rsqrt(group_mean + 1e-05)[:, None, None] * gate_norm_weight[None]).astype(

time: 252 us -> 242 us (0.960)
  blocking collectives: 95 us -> 85.2 us
    psum x1 -> x2, blocking collectives: 31.1 us -> 21.2 us  [the longest x1 18.8 us: body(): lax.psum(lax.psum(local_squares[:, None] * group_pick[None], 'section'),...]
where the time goes in v1:
time: 242 us
  waiting for transfers between devices  107 us (44%)
  blocking collectives  85.2 us (35%)
  matrix products  23.5 us (10%)
  between operations  16.2 us (7%)
  other arithmetic  9.25 us (4%)
    reduce_scatter x1, waiting for transfers between devices, body(): lax.psum_scatter(mixer_terms, ('row', 'section'), scatter_dimension=1, ti...  54.8 us
    reduce_scatter x1, waiting for transfers between devices, body(): lax.psum_scatter(down_terms, ('row', 'section'), scatter_dimension=1, til...  52.2 us
    all_gather x1, blocking collectives, body(): full_rows = lax.all_gather(hidden, ('row', 'section'), axis=1, tiled=True)  24.9 us
    all_gather x1, blocking collectives, body(): middle_full = lax.all_gather(middle, ('row', 'section'), axis=1, tiled=True)  20.9 us
    psum x1, blocking collectives, body(): lax.psum(lax.psum(local_squares[:, None] * group_pick[None], 'section'),...  18.8 us
    all_gather x1, blocking collectives, body(): all_bc = lax.all_gather(mixed_bc, ('row', 'section'), axis=1, tiled=True)  18.1 us
    dot_general x1, matrix products, body(): jnp.dot(activated, down_weight, preferred_element_type=jnp.float32)  14.8 us
  transfers between devices with their start and end apart: 2, of which 2 were waited for; matrix products, arithmetic and copies ran while one was open for 1% of the time, Pallas kernels for 0%

profile of v1, /device:TPU:0, one launch (start us, length us, event | category | flops | bytes accessed | tf_op | source)
XLA Modules:
  0.0 241.8 jit_solution(8228959861870243559)
XLA Ops:
  7.2 0.0 copy-start
  7.2 0.0 reduce-scatter.3.cloned.1.call-start
  7.3 24.9 %all_gather.9 = bf16[32,8192]{1,0:T(8,128)(2,1)S(1)} all-gather(bf16[32,512]{1,0:T(8,128)(2,1)} %param.21), channel_id=1, replica_groups=mesh['groups'=2,'row'=8,'section'=2] {'row','section'}, dimensions={1}, use_global_device_ids=true | all-gather | bytes 557056 | tf_op jit(solution)/shard_map/all_gather | solution.py:41
  32.2 0.2 fusion.4
  32.4 1.7 convolution_bitcast_fusion
  34.2 0.1 copy.32
  34.3 0.8 multiply_reduce_fusion.1
  35.0 0.1 copy.33
  35.8 0.0 copy-done
  35.8 1.2 fusion.2
  37.0 0.8 multiply_reduce_fusion
  37.8 0.7 divide_multiply_fusion
  38.4 18.1 %all_gather.10 = f32[32,2048]{1,0:T(8,128)S(1)} all-gather(f32[32,128]{1,0:T(8,128)S(1)} %divide_multiply_fusion), channel_id=1, replica_groups=mesh['groups'=2,'row'=8,'section'=2] {'row','section'}, dimensions={1}, use_global_device_ids=true | all-gather | bytes 278528 | tf_op jit(solution)/shard_map/all_gather | solution.py:58
  56.6 0.1 reshape.225
  58.1 1.1 multiply_exponential_fusion
  59.2 0.8 broadcast_multiply_fusion
  60.0 0.1 copy.34
  60.0 0.1 reshape.227
  60.1 2.3 fusion.13
  62.3 0.1 copy.36
  62.4 0.8 multiply_reduce_fusion.2
  63.2 0.1 broadcast_multiply_fusion.1
  63.3 2.5 %psum.14 = f32[32,4]{0,1:T(4,128)S(1)} all-reduce(f32[32,4]{0,1:T(4,128)S(1)} %broadcast_multiply_fusion.1), channel_id=1, replica_groups=mesh['groups'=2,'row'=8,'section'=2] {'section'}, use_global_device_ids=true, to_apply=%region_4.5 | all-reduce | flops 128 | bytes 1024 | tf_op jit(solution)/shard_map/psum | solution.py:79
  65.7 18.8 %psum.15 = f32[32,4]{0,1:T(4,128)S(1)} all-reduce(f32[32,4]{0,1:T(4,128)S(1)} %psum.14), channel_id=1, replica_groups=mesh['groups'=2,'row'=8,'section'=2] {'row'}, use_global_device_ids=true, to_apply=%region_5.6 | all-reduce | flops 128 | bytes 1024 | tf_op jit(solution)/shard_map/psum | solution.py:79
  84.5 0.1 multiply_reduce_fusion.3
  84.6 2.4 %fusion.19 = f32[32,8192]{1,0:T(8,128)} fusion(bf16[1,32,8192]{2,1,0:T(8,128)(2,1)} %param.37, f32[32,32]{0,1:T(8,128)S(1)} %get-tuple-element.5, f32[32]{0:T(128)} %bitcast.59, f32[32]{0:T(128)S(1)} %add_rsqrt_fusion.1), kind=kOutput, calls=%fused_computation.26 | convolution fusion | flops 16780288 | bytes 1577216 | tf_op jit(solution)/shard_map/dot_general | solution.py:85
  87.1 0.0 reduce-scatter.3.cloned.1.call-update
  87.1 0.0 reduce-scatter.5.cloned.1.call-start
  87.1 54.8 %reduce-scatter.3.cloned.1.call-done = f32[32,512]{1,0:T(8,128)} async-done(((f32[32,8192]{1,0:T(8,128)}), f32[32,512]{1,0:T(8,128)}) %reduce-scatter.3.cloned.1.call-update) | async-done | bytes 65552 | tf_op jit(solution)/shard_map/reduce_scatter | solution.py:90
  141.9 0.8 add_convert_fusion.1
  142.7 20.9 %all_gather.11 = bf16[32,8192]{1,0:T(8,128)(2,1)S(1)} all-gather(bf16[32,512]{1,0:T(8,128)(2,1)S(1)} %add_convert_fusion.1), channel_id=1, replica_groups=mesh['groups'=2,'row'=8,'section'=2] {'row','section'}, dimensions={1}, use_global_device_ids=true | all-gather | bytes 557056 | tf_op jit(solution)/shard_map/all_gather | solution.py:92
  163.6 0.2 fusion.9
  163.8 0.0 copy-start.4
  163.9 0.0 copy-start.2
  163.9 0.0 copy-start.3
  163.9 0.0 copy-start.1
  163.9 14.8 %fusion.16 = f32[32,8192]{1,0:T(8,128)} fusion(bf16[1024,8192]{1,0:T(8,128)(2,1)} %param.40, bf16[8192,1024]{1,0:T(8,128)(2,1)} %param.39, bf16[32,8192]{1,0:T(8,128)(2,1)S(1)} %all_gather.11, f32[8192]{0:T(1024)} %param.38, f32[32]{0:T(128)S(1)} %add_rsqrt_fusion), kind=kOutput, calls=%fused_computation.25 | convolution fusion | flops 1074888704 | bytes 35160192 | tf_op jit(solution)/shard_map/dot_general | solution.py:96
  178.6 0.0 reduce-scatter.5.cloned.1.call-update
  178.7 0.0 copy-done.4
  178.7 0.0 copy-done.2
  178.7 0.7 fusion.35
  179.4 0.0 copy-done.3
  179.4 0.7 fusion.33
  180.1 0.0 copy-done.1
  180.1 1.2 fusion.8
  181.3 52.2 %reduce-scatter.5.cloned.1.call-done = f32[32,512]{1,0:T(8,128)} async-done(((f32[32,8192]{1,0:T(8,128)}), f32[32,512]{1,0:T(8,128)}) %reduce-scatter.5.cloned.1.call-update) | async-done | bytes 65552 | tf_op jit(solution)/shard_map/reduce_scatter | solution.py:97
  233.5 1.5 add_convert_fusion
  (9 shorter events, 0.1 us)
Async XLA Ops:
  7.2 28.6 %copy-start = (bf16[8192,128]{1,0:T(8,128)(2,1)S(1)}, bf16[8192,128]{1,0:T(8,128)(2,1)}, u32[]{:S(2)}) copy-start(bf16[8192,128]{1,0:T(8,128)(2,1)} %param.24) | copy-start | bytes 6291460
  7.2 134.7 %reduce-scatter.3.cloned.1.call-start = ((), (), s32[]{:S(2)}) async-start(), calls=%async_computation.2 | async-start | bytes 1114112 | tf_op jit(solution)/shard_map/reduce_scatter | solution.py:90
  87.1 146.4 %reduce-scatter.5.cloned.1.call-start = ((), (), s32[]{:S(2)}) async-start(), calls=%async_computation.3 | async-start | bytes 1114112 | tf_op jit(solution)/shard_map/reduce_scatter | solution.py:97
  163.8 14.8 %copy-start.4 = (s32[32]{0:T(128)S(1)}, s32[32]{0:T(128)}, u32[]{:S(2)}) copy-start(s32[32]{0:T(128)} %param.41) | copy-start | bytes 388
  163.9 14.8 %copy-start.2 = (bf16[32,3,1,32]{3,0,2,1:T(8,128)(2,1)S(1)}, bf16[32,3,1,32]{3,0,2,1:T(8,128)(2,1)}, u32[]{:S(2)}) copy-start(bf16[32,3,1,32]{3,0,2,1:T(8,128)(2,1)} %param.33) | copy-start | bytes 18436
  163.9 15.5 %copy-start.3 = (bf16[32,3,128]{2,0,1:T(8,128)(2,1)S(1)}, bf16[32,3,128]{2,0,1:T(8,128)(2,1)}, u32[]{:S(2)}) copy-start(bf16[32,3,128]{2,0,1:T(8,128)(2,1)} %param.34) | copy-start | bytes 73732
  163.9 16.2 %copy-start.1 = (bf16[32,1,32,256]{3,2,1,0:T(8,128)(2,1)S(1)}, bf16[32,1,32,256]{3,2,1,0:T(8,128)(2,1)}, u32[]{:S(2)}) copy-start(bf16[32,1,32,256]{3,2,1,0:T(8,128)(2,1)} %param.35) | copy-start | bytes 1572868
Sparse Core Ops, SparseCore 0:
  87.2 54.6 reduce-scatter.2
  178.8 54.6 reduce-scatter.4
